TPU v7x, 128 devices: a whole 4x4x4 slice. The times are simulated.
128 devices in a mesh: lon: 16 (over x, y_lo, core), lat: 8 (over z, y_hi).
Axes of the slice: x: 4, y: 4 (y_hi: 2, y_lo: 2; y = y_hi * 2 + y_lo), z: 4, core: 2. Of those that a mesh axis runs over, the one named last changes fastest.
Arguments:
- heat_content_field: float32 [12, 768, 2048], P(None, 'lat', 'lon'), may hold values from -6 to 6
- saltiness_field: float32 [12, 768, 2048], P(None, 'lat', 'lon'), may hold values from -6 to 6
- eastward_cfl_number: float32 [12, 768, 2048], P(None, 'lat', 'lon'), may hold values from -0.4 to 0.4
- northward_cfl_number: float32 [12, 768, 2048], P(None, 'lat', 'lon'), may hold values from -0.4 to 0.4
- seawater_indicator: int32 [768, 2048], P('lat', 'lon'), may hold values 0 or 1
- submerged_layer_total: int32 [768, 2048], P('lat', 'lon'), may hold values from 1 to 12
- seam_partner_index: int32 [2048], replicated, may hold values from 0 to 2047, as said below
Outputs:
- new_temperature: float32 [12, 768, 2048], P(None, 'lat', 'lon')
- new_salinity: float32 [12, 768, 2048], P(None, 'lat', 'lon')
Inputs may be any that keep to these rules, and one draw needn't show every extreme that they name: Each column appears once; the map is a reflection of the columns about a pivot, seam_partner_index[i] = (s - i) mod 2048.
All inputs are finite; a program needn't handle non-finite values. No bound on the sum of `seawater_indicator` on one device may be relied on, other than what follows from the above.
Results may differ from a plain program's by a relative error of at most 0.0003.
Values sent between devices are 32-bit elements; how exact they have to be, the bound alone decides.
A program may use at most 192 MiB of HBM per device.

v0:
```python
from functools import reduce
import jax
import jax.numpy as jnp
from jax import lax
from jax.sharding import PartitionSpec as P

RATIO_FLOOR = 0.05
SLOPE_FLOOR = 0.5
SLOPE_LIMIT = 2.0
DIFFUSIVITY = 0.1
THERMAL_COEF = 0.2
HALINE_COEF = 0.8
STATE_SIGNS = (1.0, 1.0, -1.0, -1.0, 1.0)


def extended(cells, sides, width, closed):
    for axis, dim in sides:
        count = lax.axis_size(axis)
        ends = count if closed else count - 1
        head = lax.slice_in_dim(cells, 0, width, axis=dim)
        tail = lax.slice_in_dim(cells, cells.shape[dim] - width, cells.shape[dim], axis=dim)
        cells = jnp.concatenate(
            [
                lax.ppermute(tail, axis, [(i, (i + 1) % count) for i in range(ends)]),
                cells,
                lax.ppermute(head, axis, [((i + 1) % count, i) for i in range(ends)]),
            ],
            axis=dim,
        )
    return cells


def sign_column(values):
    return jnp.array(values, jnp.float32).reshape(len(values), 1, 1, 1)


def sided(core, west_col, east_col, south_row, north_row):
    width = core.shape[-1]
    height = core.shape[-2]
    lane = lax.broadcasted_iota(jnp.int32, core.shape, core.ndim - 1)
    level = lax.broadcasted_iota(jnp.int32, core.shape, core.ndim - 2)
    at_east = jnp.where(lane == width - 1, east_col, jnp.roll(core, -1, axis=-1))
    at_west = jnp.where(lane == 0, west_col, jnp.roll(core, 1, axis=-1))
    at_north = jnp.where(level == height - 1, north_row, jnp.roll(core, -1, axis=-2))
    at_south = jnp.where(level == 0, south_row, jnp.roll(core, 1, axis=-2))
    return (core, at_east, at_west, at_north, at_south)


def low_order(tracer, zonal, meridional, wet_sides):
    value_centre, value_east, value_west, value_north, value_south = tracer
    speed_centre, speed_west = (zonal[0], zonal[2])
    flow_centre, flow_south = (meridional[0], meridional[4])
    wet_centre, wet_east, wet_west, wet_north, wet_south = wet_sides
    face_east = wet_centre * wet_east
    face_west = wet_west * wet_centre
    face_north = wet_centre * wet_north
    face_south = wet_south * wet_centre
    upwind_east = face_east * (
        jnp.maximum(speed_centre, 0.0) * value_centre + jnp.minimum(speed_centre, 0.0) * value_east
    )
    upwind_west = face_west * (
        jnp.maximum(speed_west, 0.0) * value_west + jnp.minimum(speed_west, 0.0) * value_centre
    )
    upwind_north = face_north * (
        jnp.maximum(flow_centre, 0.0) * value_centre + jnp.minimum(flow_centre, 0.0) * value_north
    )
    upwind_south = face_south * (
        jnp.maximum(flow_south, 0.0) * value_south + jnp.minimum(flow_south, 0.0) * value_centre
    )
    anti_east = face_east * speed_centre * (value_centre + value_east) * 0.5 - upwind_east
    anti_west = face_west * speed_west * (value_west + value_centre) * 0.5 - upwind_west
    anti_north = face_north * flow_centre * (value_centre + value_north) * 0.5 - upwind_north
    anti_south = face_south * flow_south * (value_south + value_centre) * 0.5 - upwind_south
    upwind = value_centre - wet_centre * (upwind_east - upwind_west + upwind_north - upwind_south)
    inflow = (
        jnp.maximum(anti_west, 0.0)
        - jnp.minimum(anti_east, 0.0)
        + jnp.maximum(anti_south, 0.0)
        - jnp.minimum(anti_north, 0.0)
    )
    outflow = (
        jnp.maximum(anti_east, 0.0)
        - jnp.minimum(anti_west, 0.0)
        + jnp.maximum(anti_north, 0.0)
        - jnp.minimum(anti_south, 0.0)
    )
    anti = (anti_east, anti_west, anti_north, anti_south)
    return (upwind, anti, inflow, outflow)


def ratios(upwind_sides, wet_sides, inflow, outflow):
    value_centre, value_east, value_west, value_north, value_south = upwind_sides
    _, wet_east, wet_west, wet_north, wet_south = wet_sides
    pairs = (
        (value_east, wet_east),
        (value_west, wet_west),
        (value_north, wet_north),
        (value_south, wet_south),
    )
    candidates = [value_centre] + [
        jnp.where(beside_wet > 0.5, beside, value_centre) for beside, beside_wet in pairs
    ]
    highest = reduce(jnp.maximum, candidates)
    lowest = reduce(jnp.minimum, candidates)
    ratio_plus = jnp.minimum(1.0, (highest - value_centre) / jnp.maximum(inflow, RATIO_FLOOR))
    ratio_minus = jnp.minimum(1.0, (value_centre - lowest) / jnp.maximum(outflow, RATIO_FLOOR))
    return jnp.concatenate([ratio_plus, ratio_minus], axis=0)


def limited(ratio_sides, upwind, anti, wet_centre):
    plus_centre, plus_east, plus_west, plus_north, plus_south = [side[:2] for side in ratio_sides]
    minus_centre, minus_east, minus_west, minus_north, minus_south = [
        side[2:] for side in ratio_sides
    ]
    anti_east, anti_west, anti_north, anti_south = anti
    coef_east = jnp.where(
        anti_east >= 0.0, jnp.minimum(plus_east, minus_centre), jnp.minimum(plus_centre, minus_east)
    )
    coef_west = jnp.where(
        anti_west >= 0.0, jnp.minimum(plus_centre, minus_west), jnp.minimum(plus_west, minus_centre)
    )
    coef_north = jnp.where(
        anti_north >= 0.0,
        jnp.minimum(plus_north, minus_centre),
        jnp.minimum(plus_centre, minus_north),
    )
    coef_south = jnp.where(
        anti_south >= 0.0,
        jnp.minimum(plus_centre, minus_south),
        jnp.minimum(plus_south, minus_centre),
    )
    return upwind - wet_centre * (
        coef_east * anti_east
        - coef_west * anti_west
        + coef_north * anti_north
        - coef_south * anti_south
    )


def vertical_of(tracer, wet):
    stacked_wet = wet[:-1] * wet[1:]
    vertical = (tracer[:, 1:] - tracer[:, :-1]) * stacked_wet
    return jnp.concatenate([vertical, jnp.zeros_like(tracer[:, :1])], axis=1)


def isopycnal(values, wet_sides):
    verticals = tuple((vertical_of(tracer, wet) for tracer, wet in zip(values, wet_sides)))
    densities = tuple((HALINE_COEF * tracer[1] - THERMAL_COEF * tracer[0] for tracer in values))
    stratas = tuple(
        (HALINE_COEF * vertical[1] - THERMAL_COEF * vertical[0] for vertical in verticals)
    )

    def face_flux(first, second):
        face = wet_sides[first] * wet_sides[second]
        slope = jnp.clip(
            (densities[second] - densities[first])
            / jnp.maximum(0.5 * (stratas[first] + stratas[second]), SLOPE_FLOOR),
            -SLOPE_LIMIT,
            SLOPE_LIMIT,
        )
        return (
            DIFFUSIVITY
            * face
            * (
                values[second]
                - values[first]
                - slope * 0.5 * (verticals[first] + verticals[second])
            )
        )

    east_flux = face_flux(0, 1)
    west_flux = face_flux(2, 0)
    north_flux = face_flux(0, 3)
    south_flux = face_flux(4, 0)
    return values[0] + wet_sides[0] * (east_flux - west_flux + north_flux - south_flux)


def advance(state, sides):
    state_sides = sides(state, sign_column(STATE_SIGNS), 0)
    tracer = tuple((side[:2] for side in state_sides))
    zonal = tuple((side[2] for side in state_sides))
    meridional = tuple((side[3] for side in state_sides))
    wet_sides = tuple((side[4] for side in state_sides))
    upwind, anti, inflow, outflow = low_order(tracer, zonal, meridional, wet_sides)
    upwind_sides = sides(upwind, sign_column((1.0, 1.0)), 1)
    ratio = ratios(upwind_sides, wet_sides, inflow, outflow)
    ratio_sides = sides(ratio, sign_column((1.0, 1.0, 1.0, 1.0)), 2)
    advected = limited(ratio_sides, upwind, anti, wet_sides[0])
    advected_sides = sides(advected, sign_column((1.0, 1.0)), 3)
    return isopycnal(advected_sides, wet_sides)


def local(
    heat_content_field,
    saltiness_field,
    eastward_cfl_number,
    northward_cfl_number,
    seawater_indicator,
    submerged_layer_total,
    seam_partner_index,
):
    span = heat_content_field.shape[2]
    anchor = lax.axis_index("lon") * span
    on_top = lax.axis_index("lat") == lax.axis_size("lat") - 1
    vertical_layer = jnp.arange(heat_content_field.shape[0], dtype=jnp.int32)[:, None, None]
    submerged_indicator = (
        (seawater_indicator[None] == 1) & (vertical_layer < submerged_layer_total[None])
    ).astype(jnp.float32)
    state = jnp.stack(
        [
            heat_content_field,
            saltiness_field,
            eastward_cfl_number,
            northward_cfl_number,
            submerged_indicator,
        ]
    )
    own_columns = anchor + jnp.arange(span, dtype=jnp.int32)
    facing = jnp.take(seam_partner_index, own_columns)

    def rim_sides(stack, fold_row):
        columns = jnp.concatenate([stack[..., :1], stack[..., -1:]], axis=3)
        column_rim = extended(columns, (("lon", 3),), 1, True)
        rows = jnp.concatenate([stack[:, :, :1, :], stack[:, :, -1:, :]], axis=2)
        row_rim = extended(rows, (("lat", 2),), 1, False)
        north_row = jnp.where(on_top, fold_row, row_rim[:, :, 3:4, :])
        return sided(
            stack, column_rim[..., 0:1], column_rim[..., 3:4], row_rim[:, :, 0:1, :], north_row
        )

    def device_sides(stack, signs, segment):
        top_row = lax.all_gather(stack[:, :, -1:, :], "lon", axis=3, tiled=True)
        fold_row = jnp.take(top_row, facing, axis=3) * signs
        return rim_sides(stack, fold_row)

    final = advance(state, device_sides)
    return (final[0], final[1])


def solution(mesh):
    in_specs = (
        P(None, "lat", "lon"),
        P(None, "lat", "lon"),
        P(None, "lat", "lon"),
        P(None, "lat", "lon"),
        P("lat", "lon"),
        P("lat", "lon"),
        P(),
    )
    out_specs = (P(None, "lat", "lon"), P(None, "lat", "lon"))
    return jax.shard_map(local, mesh=mesh, in_specs=in_specs, out_specs=out_specs, check_vma=False)
```

profile of v0, /device:TPU:97, one launch (start us, length us, event | category | flops | bytes accessed | tf_op | source)
XLA Modules:
  0.0 285.5 jit_solution(14750292049172549492)
XLA Ops:
  4.7 4.7 %collective-permute-start.2 = (f32[5,12,1,128]{3,2,1,0:T(1,128)}, f32[5,12,1,128]{3,2,1,0:T(1,128)}, u32[]{:S(2)}, u32[]{:S(2)}) collective-permute-start(f32[5,12,1,128]{3,2,1,0:T(1,128)} %get-tuple-element.45), channel_id=1, source_target_pairs={{1,0},{2,1},{3,2},{4,3},{5,4},{6,5},{7,6},{9,8},{10,9},{11,10},{12... | collective-permute-start | bytes 92168 | tf_op jit(solution)/shard_map/ppermute | solution.py:26
  12.0 3.7 %fusion.105 = (f32[5,12,96,1]{3,2,1,0:T(8,128)}, f32[5,12,96,1]{3,2,1,0:T(8,128)}) fusion(f32[5,12,96,128]{3,2,1,0:T(8,128)S(1)} %convert_dynamic-update-slice_fusion), kind=kLoop, calls=%fused_computation.255 | loop fusion | bytes 92160 | tf_op jit(solution)/shard_map/slice | solution.py:222
  23.9 22.0 %all_gather.12 = f32[5,12,1,2048]{3,2,1,0:T(1,128)} all-gather(f32[5,12,1,128]{3,2,1,0:T(1,128)} %get-tuple-element.46), channel_id=1, replica_groups=mesh['lon'=16,'lat'=8] {'lon'}, dimensions={3}, use_global_device_ids=true | all-gather | bytes 522240 | tf_op jit(solution)/shard_map/all_gather | solution.py:232
  47.8 3.0 %fusion.106 = (f32[5,12,95,128]{3,2,1,0:T(8,128)}, f32[5,12,95,128]{3,2,1,0:T(8,128)}) fusion(f32[5,12,96,128]{3,2,1,0:T(8,128)S(1)} %convert_dynamic-update-slice_fusion), kind=kLoop, calls=%fused_computation.256 | loop fusion | bytes 11673600 | tf_op jit(solution)/shard_map/jit(_roll_static)/slice | solution.py:44
  50.8 3.6 %fusion.104 = (f32[5,12,96,127]{3,2,1,0:T(8,128)}, f32[5,12,96,127]{3,2,1,0:T(8,128)}) fusion(f32[5,12,96,128]{3,2,1,0:T(8,128)S(1)} %convert_dynamic-update-slice_fusion), kind=kLoop, calls=%fused_computation.254 | loop fusion | bytes 11704320 | tf_op jit(solution)/shard_map/jit(_roll_static)/slice | solution.py:42
  56.6 6.0 %copy.954 = f32[5,12,1,2048]{1,0,3,2:T(8,128)} copy(f32[5,12,1,2048]{3,2,1,0:T(1,128)} %all_gather.12) | data formatting | bytes 983040 | tf_op jit(solution)/shard_map/all_gather | solution.py:232
  62.6 4.9 %gather_fusion.1 = f32[128,5,12]{2,1,0:T(8,128)} fusion(f32[5,12,2048]{1,0,2:T(8,128)} %bitcast.128, s32[1024]{0:T(1024)} %pad_clamp_fusion.1), kind=kCustom, calls=%fused_computation.3 | custom fusion | bytes 61952 | tf_op jit(solution)/shard_map/jit(_take)/gather | solution.py:233
  70.2 3.2 %maximum_select_fusion = f32[5,12,96,128]{3,2,1,0:T(8,128)S(1)} fusion(f32[5,12,96,1]{3,2,1,0:T(8,128)S(1)} %copy-done.5, f32[5,12,96,127]{3,2,1,0:T(8,128)} %get-tuple-element.39, f32[5,12,96]{2,1,0:T(8,128)S(1)} %bitcast.143, pred[128]{0:T(512)(128)(4,1)S(1)} %get-tuple-element.98), kind=kLoop, calls=%fused_computation.19 | loop fusion | flops 1474560 | bytes 5921408 | tf_op jit(solution)/shard_map/jit(_where)/select_n | solution.py:42
  103.3 5.8 %collective-permute-start.6 = (f32[2,12,1,128]{3,2,1,0:T(1,128)}, f32[2,12,1,128]{3,2,1,0:T(1,128)}, u32[]{:S(2)}, u32[]{:S(2)}) collective-permute-start(f32[2,12,1,128]{3,2,1,0:T(1,128)} %get-tuple-element.73), channel_id=1, source_target_pairs={{1,0},{2,1},{3,2},{4,3},{5,4},{6,5},{7,6},{9,8},{10,9},{11,10},{12... | collective-permute-start | bytes 36872 | tf_op jit(solution)/shard_map/ppermute | solution.py:26
  112.8 17.1 %all_gather.13 = f32[2,12,1,2048]{3,0,2,1:T(2,128)S(1)} all-gather(f32[2,12,1,128]{3,0,2,1:T(2,128)} %copy.960), channel_id=1, replica_groups=mesh['lon'=16,'lat'=8] {'lon'}, dimensions={3}, use_global_device_ids=true | all-gather | bytes 208896 | tf_op jit(solution)/shard_map/all_gather | solution.py:232
  137.2 10.3 %fusion.12 = (f32[2,12,96,128]{3,2,1,0:T(8,128)S(1)}, f32[2,12,96,128]{3,2,1,0:T(8,128)S(1)}, f32[2,12,96,128]{3,2,1,0:T(8,128)S(1)}, f32[2,12,96,128]{3,2,1,0:T(8,128)S(1)}, f32[2,12,96,128]{3,2,1,0:T(8,128)S(1)}) fusion(f32[2,12,96,128]{3,2,1,0:T(8,128)S(1)} %multiply_subtract_fusion.4, f32[2,12,1,128]{3,2,1,0:T(1,128)} %get-tuple-element.73, ...), kind=kLoop, calls=%fused_computation.41 | loop fusion | flops 17694720 | bytes 27765184 | tf_op jit(solution)/shard_map/min | solution.py:105
  147.6 4.2 %fusion.18 = f32[2,12,96,128]{3,2,1,0:T(8,128)S(1)} fusion(f32[2,12,96,128]{3,2,1,0:T(8,128)S(1)} %multiply_subtract_fusion.4, f32[2,12,1,128]{3,2,1,0:T(1,128)} %get-tuple-element.73, f32[2,12,95,128]{3,2,1,0:T(8,128)S(1)} %copy-done.35, f32[2,12,1,128]{3,2,1,0:T(1,128)} %get-tuple-element.72, f32[2,12,96,128]{3,2,1,0:T(8,128)S(1)} %get-tuple-element.22, ...), kind=kLoop, calls=%fused_computation.47 | loop fusion | flops 7962624 | bytes 12429760 | tf_op jit(solution)/shard_map/min | solution.py:106
  151.8 3.0 %fusion.1 = (f32[4,12,96,1]{3,2,1,0:T(8,128)}, f32[4,12,96,1]{3,2,1,0:T(8,128)}) fusion(f32[2,12,96,128]{3,2,1,0:T(8,128)S(1)} %get-tuple-element.18, f32[2,12,96,128]{3,2,1,0:T(8,128)S(1)} %fusion.18), kind=kLoop, calls=%fused_computation.24 | loop fusion | flops 9216 | bytes 2396160 | tf_op jit(solution)/shard_map/concatenate | solution.py:107
  154.8 3.0 %fusion.2 = (f32[4,12,96,127]{3,2,1,0:T(8,128)}, f32[4,12,96,127]{3,2,1,0:T(8,128)}) fusion(f32[2,12,96,128]{3,2,1,0:T(8,128)S(1)} %get-tuple-element.18, f32[2,12,96,128]{3,2,1,0:T(8,128)S(1)} %fusion.18), kind=kLoop, calls=%fused_computation.25 | loop fusion | flops 1170432 | bytes 7041024 | tf_op jit(solution)/shard_map/concatenate | solution.py:107
  171.1 19.1 %all_gather.14 = f32[4,12,1,2048]{3,0,2,1:T(4,128)} all-gather(f32[4,12,1,128]{3,0,2,1:T(4,128)} %copy.972), channel_id=1, replica_groups=mesh['lon'=16,'lat'=8] {'lon'}, dimensions={3}, use_global_device_ids=true | all-gather | bytes 417792 | tf_op jit(solution)/shard_map/all_gather | solution.py:232
  190.3 4.6 %copy.973 = f32[4,12,1,2048]{1,0,3,2:T(4,128)} copy(f32[4,12,1,2048]{3,0,2,1:T(4,128)} %all_gather.14) | data formatting | bytes 786432 | tf_op jit(solution)/shard_map/all_gather | solution.py:232
  194.8 3.8 %gather_fusion.2 = f32[128,4,12]{2,1,0:T(4,128)} fusion(f32[4,12,2048]{1,0,2:T(4,128)} %bitcast.133, s32[1024]{0:T(1024)} %pad_clamp_fusion.1), kind=kCustom, calls=%fused_computation.4 | custom fusion | bytes 49664 | tf_op jit(solution)/shard_map/jit(_take)/gather | solution.py:233
  200.3 6.1 %collective-permute-start.10 = (f32[4,12,1,128]{3,2,1,0:T(1,128)}, f32[4,12,1,128]{3,2,1,0:T(1,128)S(1)}, u32[]{:S(2)}, u32[]{:S(2)}) collective-permute-start(f32[4,12,1,128]{3,2,1,0:T(1,128)} %get-tuple-element.51), channel_id=1, source_target_pairs={{1,0},{2,1},{3,2},{4,3},{5,4},{6,5},{7,6},{9,8},{10,9},{11,10},{12... | collective-permute-start | bytes 73736 | tf_op jit(solution)/shard_map/ppermute | solution.py:26
  207.9 3.2 %maximum_select_fusion.4 = f32[4,12,96,128]{3,2,1,0:T(8,128)S(1)} fusion(f32[4,12,96,1]{3,2,1,0:T(8,128)} %get-tuple-element.49, f32[4,12,96,127]{3,2,1,0:T(8,128)} %get-tuple-element.47, f32[4,12,96]{2,1,0:T(8,128)S(1)} %copy.969, pred[128]{0:T(512)(128)(4,1)S(1)} %get-tuple-element.98), kind=kLoop, calls=%fused_computation.31 | loop fusion | flops 1179648 | bytes 4737152 | tf_op jit(solution)/shard_map/jit(_where)/select_n | solution.py:42
  233.7 18.5 %all_gather.15 = f32[2,12,1,2048]{3,0,2,1:T(2,128)} all-gather(f32[2,12,1,128]{3,0,2,1:T(2,128)} %copy.984), channel_id=1, replica_groups=mesh['lon'=16,'lat'=8] {'lon'}, dimensions={3}, use_global_device_ids=true | all-gather | bytes 208896 | tf_op jit(solution)/shard_map/all_gather | solution.py:232
  252.3 3.7 %copy.985 = f32[2,12,2048]{1,0,2:T(2,128)} copy(f32[2,12,2048]{2,0,1:T(2,128)} %bitcast.135) | data formatting | bytes 393216 | tf_op jit(solution)/shard_map/jit(_take)/Arg_0.21 | solution.py:233
  255.9 3.1 %gather_fusion.4 = f32[128,2,12]{2,1,0:T(2,128)} fusion(f32[2,12,2048]{1,0,2:T(2,128)} %copy.985, s32[1024]{0:T(1024)} %pad_clamp_fusion), kind=kCustom, calls=%fused_computation.1.clone | custom fusion | bytes 25088 | tf_op jit(solution)/shard_map/jit(_take)/gather | solution.py:233
  260.6 5.8 %collective-permute-start.14 = (f32[2,12,1,128]{3,2,1,0:T(1,128)}, f32[2,12,1,128]{3,2,1,0:T(1,128)S(1)}, u32[]{:S(2)}, u32[]{:S(2)}) collective-permute-start(f32[2,12,1,128]{3,2,1,0:T(1,128)} %get-tuple-element.64), channel_id=1, source_target_pairs={{1,0},{2,1},{3,2},{4,3},{5,4},{6,5},{7,6},{9,8},{10,9},{11,10},{12... | collective-permute-start | bytes 36872 | tf_op jit(solution)/shard_map/ppermute | solution.py:26
  280.6 3.8 %multiply_add_fusion = f32[2,12,96,128]{3,2,1,0:T(8,128)S(1)} fusion(f32[2,12,96,128]{3,2,1,0:T(8,128)S(1)} %fusion.23, f32[2,11,96,128]{3,2,1,0:T(8,128)S(1)} %fusion.35, f32[2,11,96,128]{3,2,1,0:T(8,128)S(1)} %fusion.36, f32[2,11,96,128]{3,2,1,0:T(8,128)S(1)} %fusion.37, f32[2,11,96,128]{3,2,1,0:T(8,128)S(1)} %fusion.38, ...), kind=kLoop, calls=%fused_computation.81 | loop fusion | flops 9732096 | bytes 17836480 | tf_op jit(solution)/shard_map/add | solution.py:175
  (309 shorter events, 117.3 us)
Async XLA Ops:
  0.6 45.4 %copy-start = (s32[2048]{0:T(1024)S(1)}, s32[2048]{0:T(1024)}, u32[]{:S(2)}) copy-start(s32[2048]{0:T(1024)} %param.19) | copy-start | bytes 24580
  4.7 74.9 %collective-permute-start.2 = (f32[5,12,1,128]{3,2,1,0:T(1,128)}, f32[5,12,1,128]{3,2,1,0:T(1,128)}, u32[]{:S(2)}, u32[]{:S(2)}) collective-permute-start(f32[5,12,1,128]{3,2,1,0:T(1,128)} %get-tuple-element.45), channel_id=1, source_target_pairs={{1,0},{2,1},{3,2},{4,3},{5,4},{6,5},{7,6},{9,8},{10,9},{11,10},{12... | collective-permute-start | bytes 92168 | tf_op jit(solution)/shard_map/ppermute | solution.py:26
  9.3 74.0 %collective-permute-start.3 = (f32[5,12,1,128]{3,2,1,0:T(1,128)}, f32[5,12,1,128]{3,2,1,0:T(1,128)}, u32[]{:S(2)}, u32[]{:S(2)}) collective-permute-start(f32[5,12,1,128]{3,2,1,0:T(1,128)} %get-tuple-element.46), channel_id=1, source_target_pairs={{0,1},{1,2},{2,3},{3,4},{4,5},{5,6},{6,7},{8,9},{9,10},{10,11},{11... | collective-permute-start | bytes 92168 | tf_op jit(solution)/shard_map/ppermute | solution.py:24
  18.6 50.8 %collective-permute-start = (f32[5,12,96,1]{2,3,1,0:T(1,128)}, f32[5,12,96,1]{2,3,1,0:T(1,128)}, u32[]{:S(2)}, u32[]{:S(2)}) collective-permute-start(f32[5,12,96,1]{2,3,1,0:T(1,128)} %copy.952), channel_id=1, source_target_pairs={{8,0},{16,8},{24,16},{32,24},{40,32},{48,40},{56,48},{64,56},{72,6... | collective-permute-start | bytes 69128 | tf_op jit(solution)/shard_map/ppermute | solution.py:26
  22.7 52.5 %collective-permute-start.1 = (f32[5,12,96,1]{2,3,1,0:T(1,128)}, f32[5,12,96,1]{2,3,1,0:T(1,128)}, u32[]{:S(2)}, u32[]{:S(2)}) collective-permute-start(f32[5,12,96,1]{2,3,1,0:T(1,128)} %copy.953), channel_id=1, source_target_pairs={{0,8},{8,16},{16,24},{24,32},{32,40},{40,48},{48,56},{56,64},{64,7... | collective-permute-start | bytes 69128 | tf_op jit(solution)/shard_map/ppermute | solution.py:24
  54.5 35.1 %copy-start.11 = (f32[12,96,128]{2,1,0:T(8,128)}, f32[12,96,128]{2,1,0:T(8,128)S(1)}, u32[]{:S(2)}) copy-start(f32[12,96,128]{2,1,0:T(8,128)S(1)} %fusion.83) | copy-start | bytes 1769476
  56.6 211.3 %copy-start.83 = (pred[128]{0:T(512)(128)(4,1)}, pred[128]{0:T(512)(128)(4,1)S(1)}, u32[]{:S(2)}) copy-start(pred[128]{0:T(512)(128)(4,1)S(1)} %get-tuple-element.98) | copy-start | bytes 388
  56.6 213.4 %copy-start.81 = (pred[128]{0:T(512)(128)(4,1)}, pred[128]{0:T(512)(128)(4,1)S(1)}, u32[]{:S(2)}) copy-start(pred[128]{0:T(512)(128)(4,1)S(1)} %get-tuple-element.97) | copy-start | bytes 388
  81.9 19.7 %copy-start.6 = (f32[5,12,96,128]{3,2,1,0:T(8,128)}, f32[5,12,96,128]{3,2,1,0:T(8,128)S(1)}, u32[]{:S(2)}) copy-start(f32[5,12,96,128]{3,2,1,0:T(8,128)S(1)} %maximum_select_fusion.2) | copy-start | bytes 8847364
  92.8 18.0 %copy-start.15 = (f32[2,12,96,1]{3,2,1,0:T(8,128)}, f32[2,12,96,1]{3,2,1,0:T(8,128)S(1)}, u32[]{:S(2)}) copy-start(f32[2,12,96,1]{3,2,1,0:T(8,128)S(1)} %get-tuple-element.69) | copy-start | bytes 27652
  92.8 44.3 %copy-start.14 = (f32[2,12,96,1]{3,2,1,0:T(8,128)}, f32[2,12,96,1]{3,2,1,0:T(8,128)S(1)}, u32[]{:S(2)}) copy-start(f32[2,12,96,1]{3,2,1,0:T(8,128)S(1)} %get-tuple-element.68) | copy-start | bytes 27652
  98.0 38.3 %collective-permute-start.7 = (f32[2,12,1,128]{3,2,1,0:T(1,128)}, f32[2,12,1,128]{3,2,1,0:T(1,128)}, u32[]{:S(2)}, u32[]{:S(2)}) collective-permute-start(f32[2,12,1,128]{3,2,1,0:T(1,128)} %get-tuple-element.72), channel_id=1, source_target_pairs={{0,1},{1,2},{2,3},{3,4},{4,5},{5,6},{6,7},{8,9},{9,10},{10,11},{11... | collective-permute-start | bytes 36872 | tf_op jit(solution)/shard_map/ppermute | solution.py:24
  103.3 32.2 %collective-permute-start.6 = (f32[2,12,1,128]{3,2,1,0:T(1,128)}, f32[2,12,1,128]{3,2,1,0:T(1,128)}, u32[]{:S(2)}, u32[]{:S(2)}) collective-permute-start(f32[2,12,1,128]{3,2,1,0:T(1,128)} %get-tuple-element.73), channel_id=1, source_target_pairs={{1,0},{2,1},{3,2},{4,3},{5,4},{6,5},{7,6},{9,8},{10,9},{11,10},{12... | collective-permute-start | bytes 36872 | tf_op jit(solution)/shard_map/ppermute | solution.py:26
  110.1 24.7 %collective-permute-start.4 = (f32[2,12,96,1]{2,0,3,1:T(2,128)}, f32[2,12,96,1]{2,0,3,1:T(2,128)}, u32[]{:S(2)}, u32[]{:S(2)}) collective-permute-start(f32[2,12,96,1]{2,0,3,1:T(2,128)} %copy.956), channel_id=1, source_target_pairs={{8,0},{16,8},{24,16},{32,24},{40,32},{48,40},{56,48},{64,56},{72,6... | collective-permute-start | bytes 27656 | tf_op jit(solution)/shard_map/ppermute | solution.py:26
  111.8 23.8 %collective-permute-start.5 = (f32[2,12,96,1]{2,0,3,1:T(2,128)}, f32[2,12,96,1]{2,0,3,1:T(2,128)S(1)}, u32[]{:S(2)}, u32[]{:S(2)}) collective-permute-start(f32[2,12,96,1]{2,0,3,1:T(2,128)} %copy.958), channel_id=1, source_target_pairs={{0,8},{8,16},{16,24},{24,32},{32,40},{40,48},{48,56},{56,64},{64,7... | collective-permute-start | bytes 27656 | tf_op jit(solution)/shard_map/ppermute | solution.py:24
  151.8 62.1 %copy-start.2 = (f32[2,12,96,128]{3,2,1,0:T(8,128)}, f32[2,12,96,128]{3,2,1,0:T(8,128)S(1)}, u32[]{:S(2)}) copy-start(f32[2,12,96,128]{3,2,1,0:T(8,128)S(1)} %fusion.18) | copy-start | bytes 3538948
  161.5 51.7 %collective-permute-start.11 = (f32[4,12,1,128]{3,2,1,0:T(1,128)}, f32[4,12,1,128]{3,2,1,0:T(1,128)}, u32[]{:S(2)}, u32[]{:S(2)}) collective-permute-start(f32[4,12,1,128]{3,2,1,0:T(1,128)} %get-tuple-element.52), channel_id=1, source_target_pairs={{0,1},{1,2},{2,3},{3,4},{4,5},{5,6},{6,7},{8,9},{9,10},{10,11},{11... | collective-permute-start | bytes 73736 | tf_op jit(solution)/shard_map/ppermute | solution.py:24
  166.4 40.0 %collective-permute-start.8 = (f32[4,12,96,1]{2,0,3,1:T(4,128)}, f32[4,12,96,1]{2,0,3,1:T(4,128)}, u32[]{:S(2)}, u32[]{:S(2)}) collective-permute-start(f32[4,12,96,1]{2,0,3,1:T(4,128)} %copy.968), channel_id=1, source_target_pairs={{8,0},{16,8},{24,16},{32,24},{40,32},{48,40},{56,48},{64,56},{72,6... | collective-permute-start | bytes 55304 | tf_op jit(solution)/shard_map/ppermute | solution.py:26
  169.6 37.6 %collective-permute-start.9 = (f32[4,12,96,1]{2,0,3,1:T(4,128)}, f32[4,12,96,1]{2,0,3,1:T(4,128)}, u32[]{:S(2)}, u32[]{:S(2)}) collective-permute-start(f32[4,12,96,1]{2,0,3,1:T(4,128)} %copy.970), channel_id=1, source_target_pairs={{0,8},{8,16},{16,24},{24,32},{32,40},{40,48},{48,56},{56,64},{64,7... | collective-permute-start | bytes 55304 | tf_op jit(solution)/shard_map/ppermute | solution.py:24
  200.3 12.8 %collective-permute-start.10 = (f32[4,12,1,128]{3,2,1,0:T(1,128)}, f32[4,12,1,128]{3,2,1,0:T(1,128)S(1)}, u32[]{:S(2)}, u32[]{:S(2)}) collective-permute-start(f32[4,12,1,128]{3,2,1,0:T(1,128)} %get-tuple-element.51), channel_id=1, source_target_pairs={{1,0},{2,1},{3,2},{4,3},{5,4},{6,5},{7,6},{9,8},{10,9},{11,10},{12... | collective-permute-start | bytes 73736 | tf_op jit(solution)/shard_map/ppermute | solution.py:26
  225.9 48.3 %collective-permute-start.15 = (f32[2,12,1,128]{3,2,1,0:T(1,128)}, f32[2,12,1,128]{3,2,1,0:T(1,128)}, u32[]{:S(2)}, u32[]{:S(2)}) collective-permute-start(f32[2,12,1,128]{3,2,1,0:T(1,128)} %get-tuple-element.65), channel_id=1, source_target_pairs={{0,1},{1,2},{2,3},{3,4},{4,5},{5,6},{6,7},{8,9},{9,10},{10,11},{11... | collective-permute-start | bytes 36872 | tf_op jit(solution)/shard_map/ppermute | solution.py:24
  228.8 37.6 %collective-permute-start.12 = (f32[2,12,96,1]{2,0,3,1:T(2,128)}, f32[2,12,96,1]{2,0,3,1:T(2,128)}, u32[]{:S(2)}, u32[]{:S(2)}) collective-permute-start(f32[2,12,96,1]{2,0,3,1:T(2,128)} %copy.980), channel_id=1, source_target_pairs={{8,0},{16,8},{24,16},{32,24},{40,32},{48,40},{56,48},{64,56},{72,6... | collective-permute-start | bytes 27656 | tf_op jit(solution)/shard_map/ppermute | solution.py:26
  232.4 34.7 %collective-permute-start.13 = (f32[2,12,96,1]{2,0,3,1:T(2,128)}, f32[2,12,96,1]{2,0,3,1:T(2,128)}, u32[]{:S(2)}, u32[]{:S(2)}) collective-permute-start(f32[2,12,96,1]{2,0,3,1:T(2,128)} %copy.982), channel_id=1, source_target_pairs={{0,8},{8,16},{16,24},{24,32},{32,40},{40,48},{48,56},{56,64},{64,7... | collective-permute-start | bytes 27656 | tf_op jit(solution)/shard_map/ppermute | solution.py:24
  260.6 13.4 %collective-permute-start.14 = (f32[2,12,1,128]{3,2,1,0:T(1,128)}, f32[2,12,1,128]{3,2,1,0:T(1,128)S(1)}, u32[]{:S(2)}, u32[]{:S(2)}) collective-permute-start(f32[2,12,1,128]{3,2,1,0:T(1,128)} %get-tuple-element.64), channel_id=1, source_target_pairs={{1,0},{2,1},{3,2},{4,3},{5,4},{6,5},{7,6},{9,8},{10,9},{11,10},{12... | collective-permute-start | bytes 36872 | tf_op jit(solution)/shard_map/ppermute | solution.py:26
  (82 other events, 321.9 us)
where the time goes:
time: 288 us; the launch traced here: 286 us
  local copies, waits for them, and re-layouts  99.8 us (35%)
  blocking collectives  76.8 us (27%)
  other arithmetic  68.2 us (24%)
  starting transfers between devices  38.6 us (13%)
    all_gather x4, blocking collectives, device_sides(): top_row = lax.all_gather(stack[:, :, -1:, :], 'lon', axis=3, tiled=True)  76.8 us
    ppermute x8, starting transfers between devices, extended(): lax.ppermute(head, axis, [((i + 1) % count, i) for i in range(ends)])  24.9 us
    slice x11, local copies, waits for them, and re-layouts, rim_sides(): columns = jnp.concatenate([stack[..., :1], stack[..., -1:]], axis=3)  20.1 us
    gather x8, local copies, waits for them, and re-layouts, device_sides(): fold_row = jnp.take(top_row, facing, axis=3) * signs  19.4 us
    unnamed x188, local copies, waits for them, and re-layouts  15.6 us
    ppermute x8, starting transfers between devices, extended(): lax.ppermute(tail, axis, [(i, (i + 1) % count) for i in range(ends)])  13.7 us
    all_gather x3, local copies, waits for them, and re-layouts, device_sides(): top_row = lax.all_gather(stack[:, :, -1:, :], 'lon', axis=3, tiled=True)  12.9 us
    min x1, other arithmetic, ratios(): jnp.minimum(1.0, (highest - value_centre) / jnp.maximum(inflow, RATIO_FLO...  10.3 us
  transfers between devices with their start and end apart: 16, of which 0 were waited for; matrix products, arithmetic and copies ran while one was open for 34% of the time, Pallas kernels for 0%

commit v1 on v0

--- a/solution.py
+++ b/solution.py
@@ -229,7 +229,11 @@
         )
 
     def device_sides(stack, signs, segment):
-        top_row = lax.all_gather(stack[:, :, -1:, :], "lon", axis=3, tiled=True)
+        x = stack[:, :, -1:, :]
+        size = lax.axis_size("lon")
+        shards = jnp.stack([x for _ in range(size)])
+        shards = lax.all_to_all(shards, "lon", split_axis=0, concat_axis=0)
+        top_row = jnp.concatenate(shards, axis=3)
         fold_row = jnp.take(top_row, facing, axis=3) * signs
         return rim_sides(stack, fold_row)
 

time: 288 us -> 269 us (0.934)
  blocking collectives: 76.8 us -> 0 us
  starting transfers between devices: 38.6 us -> 68.5 us
  other arithmetic: 68.2 us -> 90.7 us
  local copies, waits for them, and re-layouts: 99.8 us -> 105 us
    all_gather x4 -> x0, blocking collectives: 76.8 us -> none  [device_sides(): top_row = lax.all_gather(stack[:, :, -1:, :], 'lon', axis=3, tiled=True)]
    all_to_all x0 -> x4, starting transfers between devices: none -> 24.6 us  [device_sides(): shards = lax.all_to_all(shards, 'lon', split_axis=0, concat_axis=0)]
    unnamed x188 -> x222, local copies, waits for them, and re-layouts: 15.6 us -> 28.9 us
    reshape x0 -> x4, local copies, waits for them, and re-layouts: none -> 12.9 us  [device_sides(): top_row = jnp.concatenate(shards, axis=3)]
    all_gather x3 -> x0, local copies, waits for them, and re-layouts: 12.9 us -> none  [device_sides(): top_row = lax.all_gather(stack[:, :, -1:, :], 'lon', axis=3, tiled=True)]
    slice x11 -> x7, local copies, waits for them, and re-layouts: 20.1 us -> 8.37 us  [rim_sides(): columns = jnp.concatenate([stack[..., :1], stack[..., -1:]], axis=3)]
    select_n x3, other arithmetic: 1.97 us -> 6.33 us  [sided(): jnp.where(level == height - 1, north_row, jnp.roll(core, -1, axis=-2))]
    gather x8 -> x7, local copies, waits for them, and re-layouts: 19.4 us -> 15.4 us  [device_sides(): fold_row = jnp.take(top_row, facing, axis=3) * signs]
  transfers between devices with their start and end apart: 16 -> 20, of which waited for: 0 -> 0; matrix products, arithmetic and copies ran while one was open for 34% -> 43% of each run, Pallas kernels for 0% -> 0%
where the time goes in v1:
time: 269 us; the launch traced here: 266 us
  local copies, waits for them, and re-layouts  105 us (39%)
  other arithmetic  90.7 us (34%)
  starting transfers between devices  68.5 us (25%)
    unnamed x222, local copies, waits for them, and re-layouts  28.9 us
    ppermute x8, starting transfers between devices, extended(): lax.ppermute(head, axis, [((i + 1) % count, i) for i in range(ends)])  26.2 us
    all_to_all x4, starting transfers between devices, device_sides(): shards = lax.all_to_all(shards, 'lon', split_axis=0, concat_axis=0)  24.6 us
    ppermute x8, starting transfers between devices, extended(): lax.ppermute(tail, axis, [(i, (i + 1) % count) for i in range(ends)])  17.7 us
    gather x7, local copies, waits for them, and re-layouts, device_sides(): fold_row = jnp.take(top_row, facing, axis=3) * signs  15.4 us
    reshape x4, local copies, waits for them, and re-layouts, device_sides(): top_row = jnp.concatenate(shards, axis=3)  12.9 us
    min x1, other arithmetic, ratios(): jnp.minimum(1.0, (highest - value_centre) / jnp.maximum(inflow, RATIO_FLO...  10.3 us
    select_n x3, other arithmetic, sided(): jnp.where(lane == width - 1, east_col, jnp.roll(core, -1, axis=-1))  9.95 us
  transfers between devices with their start and end apart: 20, of which 0 were waited for; matrix products, arithmetic and copies ran while one was open for 43% of the time, Pallas kernels for 0%

profile of v1, /device:TPU:97, one launch (start us, length us, event | category | flops | bytes accessed | tf_op | source)
XLA Modules:
  0.0 266.1 jit_solution(12086486455971761519)
XLA Ops:
  4.6 4.8 %collective-permute-start.3 = (f32[5,12,1,128]{3,2,1,0:T(1,128)}, f32[5,12,1,128]{3,2,1,0:T(1,128)}, u32[]{:S(2)}, u32[]{:S(2)}) collective-permute-start(f32[5,12,1,128]{3,2,1,0:T(1,128)} %get-tuple-element.38), channel_id=1, source_target_pairs={{0,1},{1,2},{2,3},{3,4},{4,5},{5,6},{6,7},{8,9},{9,10},{10,11},{11... | collective-permute-start | bytes 92168 | tf_op jit(solution)/shard_map/ppermute | solution.py:24
  11.3 5.4 %all-to-all-start = ((f32[16,5,12,1,128]{4,3,2,1,0:T(1,128)}), f32[16,5,12,1,128]{4,3,2,1,0:T(1,128)}, u32[]{:S(2)}, u32[]{:S(2)}) async-start(f32[16,5,12,1,128]{4,3,2,1,0:T(1,128)} %stack.26), calls=%async_computation | async-start | bytes 983040 | tf_op jit(solution)/shard_map/all_to_all | solution.py:235
  17.6 4.4 %collective-permute-start.2 = (f32[5,12,1,128]{1,0,3,2:T(8,128)}, f32[5,12,1,128]{1,0,3,2:T(8,128)}, u32[]{:S(2)}, u32[]{:S(2)}) collective-permute-start(f32[5,12,1,128]{1,0,3,2:T(8,128)} %copy.309), channel_id=1, source_target_pairs={{1,0},{2,1},{3,2},{4,3},{5,4},{6,5},{7,6},{9,8},{10,9},{11,10},{12... | collective-permute-start | bytes 92168 | tf_op jit(solution)/shard_map/ppermute | solution.py:26
  22.0 3.7 %fusion.109 = (f32[5,12,96,1]{3,2,1,0:T(8,128)}, f32[5,12,96,1]{3,2,1,0:T(8,128)}) fusion(f32[5,12,96,128]{3,2,1,0:T(8,128)S(1)} %convert_dynamic-update-slice_fusion), kind=kLoop, calls=%fused_computation.257 | loop fusion | bytes 92160 | tf_op jit(solution)/shard_map/slice | solution.py:222
  25.7 3.6 %copy.307 = f32[5,12,96,1]{2,1,0,3:T(8,128)} copy(f32[5,12,96,1]{3,2,1,0:T(8,128)} %get-tuple-element.33) | data formatting | bytes 46080
  39.6 3.8 %fusion.108 = (f32[5,12,96,127]{3,2,1,0:T(8,128)}, f32[5,12,96,127]{3,2,1,0:T(8,128)}) fusion(f32[5,12,96,128]{3,2,1,0:T(8,128)S(1)} %convert_dynamic-update-slice_fusion), kind=kLoop, calls=%fused_computation.256 | loop fusion | bytes 11704320 | tf_op jit(solution)/shard_map/jit(_roll_static)/slice | solution.py:42
  45.5 3.7 %maximum_select_fusion = f32[5,12,96,128]{3,2,1,0:T(8,128)S(1)} fusion(f32[5,12,96,1]{3,2,1,0:T(8,128)} %get-tuple-element.33, f32[5,12,96,127]{3,2,1,0:T(8,128)} %get-tuple-element.31, f32[5,12,96]{2,1,0:T(8,128)} %bitcast.4, pred[128]{0:T(512)(128)(4,1)S(1)} %get-tuple-element.90), kind=kLoop, calls=%fused_computation.19 | loop fusion | flops 1474560 | bytes 5921408 | tf_op jit(solution)/shard_map/jit(_where)/select_n | solution.py:42
  59.7 5.8 %copy.295 = f32[5,12,1,16,128]{1,0,4,3,2:T(8,128)} copy(f32[5,12,1,16,128]{4,2,1,0,3:T(1,128)} %bitcast.11) | data formatting | bytes 983040 | tf_op jit(solution)/shard_map/reshape | solution.py:236
  65.6 4.9 %gather_fusion.1 = f32[128,5,12]{2,1,0:T(8,128)} fusion(f32[5,12,2048]{1,0,2:T(8,128)} %bitcast.155, s32[1024]{0:T(1024)} %pad_clamp_fusion.1), kind=kCustom, calls=%fused_computation.3 | custom fusion | bytes 61952 | tf_op jit(solution)/shard_map/jit(_take)/gather | solution.py:237
  91.4 3.8 %collective-permute-start.7 = (f32[2,12,1,128]{3,2,1,0:T(1,128)}, f32[2,12,1,128]{3,2,1,0:T(1,128)}, u32[]{:S(2)}, u32[]{:S(2)}) collective-permute-start(f32[2,12,1,128]{3,2,1,0:T(1,128)} %get-tuple-element.64), channel_id=1, source_target_pairs={{0,1},{1,2},{2,3},{3,4},{4,5},{5,6},{6,7},{8,9},{9,10},{10,11},{11... | collective-permute-start | bytes 36872 | tf_op jit(solution)/shard_map/ppermute | solution.py:24
  96.9 6.5 %all-to-all-start.1 = ((f32[16,2,12,1,128]{4,3,2,1,0:T(1,128)}), f32[16,2,12,1,128]{4,3,2,1,0:T(1,128)}, u32[]{:S(2)}, u32[]{:S(2)}) async-start(f32[16,2,12,1,128]{4,3,2,1,0:T(1,128)} %stack.27), calls=%async_computation.1 | async-start | bytes 393216 | tf_op jit(solution)/shard_map/all_to_all | solution.py:235
  103.4 4.6 %collective-permute-start.6 = (f32[2,12,1,128]{3,2,1,0:T(1,128)}, f32[2,12,1,128]{3,2,1,0:T(1,128)}, u32[]{:S(2)}, u32[]{:S(2)}) collective-permute-start(f32[2,12,1,128]{3,2,1,0:T(1,128)} %get-tuple-element.65), channel_id=1, source_target_pairs={{1,0},{2,1},{3,2},{4,3},{5,4},{6,5},{7,6},{9,8},{10,9},{11,10},{12... | collective-permute-start | bytes 36872 | tf_op jit(solution)/shard_map/ppermute | solution.py:26
  123.6 10.3 %fusion.12 = (f32[2,12,96,128]{3,2,1,0:T(8,128)S(1)}, f32[2,12,96,128]{3,2,1,0:T(8,128)S(1)}, f32[2,12,96,128]{3,2,1,0:T(8,128)S(1)}, f32[2,12,96,128]{3,2,1,0:T(8,128)S(1)}, f32[2,12,96,128]{3,2,1,0:T(8,128)S(1)}) fusion(f32[2,12,96,128]{3,2,1,0:T(8,128)S(1)} %multiply_subtract_fusion.4, f32[2,12,1,128]{3,2,1,0:T(1,128)} %get-tuple-element.65, ...), kind=kLoop, calls=%fused_computation.41 | loop fusion | flops 17694720 | bytes 27765184 | tf_op jit(solution)/shard_map/min | solution.py:105
  134.1 4.1 %fusion.18 = f32[2,12,96,128]{3,2,1,0:T(8,128)S(1)} fusion(f32[2,12,96,128]{3,2,1,0:T(8,128)S(1)} %multiply_subtract_fusion.4, f32[2,12,1,128]{3,2,1,0:T(1,128)S(1)} %copy-done.96, f32[2,12,95,128]{3,2,1,0:T(8,128)S(1)} %copy-done.39, f32[2,12,1,128]{3,2,1,0:T(1,128)} %get-tuple-element.64, f32[2,12,96,128]{3,2,1,0:T(8,128)S(1)} %get-tuple-element.14, ...), kind=kLoop, calls=%fused_computation.47 | loop fusion | flops 7962624 | bytes 12429760 | tf_op jit(solution)/shard_map/min | solution.py:106
  149.0 3.9 %collective-permute-start.8 = (f32[4,12,96,1]{2,0,3,1:T(4,128)}, f32[4,12,96,1]{2,0,3,1:T(4,128)}, u32[]{:S(2)}, u32[]{:S(2)}) collective-permute-start(f32[4,12,96,1]{2,0,3,1:T(4,128)} %copy.310), channel_id=1, source_target_pairs={{8,0},{16,8},{24,16},{32,24},{40,32},{48,40},{56,48},{64,56},{72,6... | collective-permute-start | bytes 55304 | tf_op jit(solution)/shard_map/ppermute | solution.py:26
  161.3 6.1 %all-to-all-start.2 = ((f32[16,4,12,1,128]{4,1,2,3,0:T(4,128)}), f32[16,4,12,1,128]{4,1,2,3,0:T(4,128)}, u32[]{:S(2)}, u32[]{:S(2)}) async-start(f32[16,4,12,1,128]{4,1,2,3,0:T(4,128)} %stack.28), calls=%async_computation.2 | async-start | bytes 786432 | tf_op jit(solution)/shard_map/all_to_all | solution.py:235
  168.7 5.7 %collective-permute-start.10 = (f32[4,12,1,128]{3,0,1,2:T(4,128)}, f32[4,12,1,128]{3,0,1,2:T(4,128)}, u32[]{:S(2)}, u32[]{:S(2)}) collective-permute-start(f32[4,12,1,128]{3,0,1,2:T(4,128)} %copy.312), channel_id=1, source_target_pairs={{1,0},{2,1},{3,2},{4,3},{5,4},{6,5},{7,6},{9,8},{10,9},{11,10},{12... | collective-permute-start | bytes 73736 | tf_op jit(solution)/shard_map/ppermute | solution.py:26
  175.8 4.2 %maximum_select_fusion.4 = f32[4,12,96,128]{3,2,1,0:T(8,128)} fusion(f32[4,12,96,1]{3,2,1,0:T(8,128)} %get-tuple-element.41, f32[4,12,96,127]{3,2,1,0:T(8,128)} %get-tuple-element.39, f32[4,12,96]{2,1,0:T(8,128)S(1)} %copy.266, pred[128]{0:T(512)(128)(4,1)S(1)} %get-tuple-element.90), kind=kLoop, calls=%fused_computation.31 | loop fusion | flops 1179648 | bytes 4737152 | tf_op jit(solution)/shard_map/jit(_where)/select_n | solution.py:42
  186.1 4.5 %copy.299 = f32[4,12,1,16,128]{1,0,4,3,2:T(4,128)} copy(f32[4,12,1,16,128]{4,0,1,2,3:T(4,128)} %bitcast.42) | data formatting | bytes 786432 | tf_op jit(solution)/shard_map/reshape | solution.py:236
  197.5 4.5 %fusion.23 = f32[2,12,96,128]{3,2,1,0:T(8,128)S(1)} fusion(f32[2,12,96,128]{3,2,1,0:T(8,128)S(1)} %multiply_subtract_fusion.4, f32[2,12,96,128]{3,2,1,0:T(8,128)} %copy-done.29, f32[2,12,96,128]{3,2,1,0:T(8,128)S(1)} %copy-done.3, f32[4,12,96,128]{3,2,1,0:T(8,128)} %fusion.6, f32[2,12,96,128]{3,2,1,0:T(8,128)S(1)} %get-tuple-element.10, ...), kind=kLoop, calls=%fused_computation.53 | loop fusion | flops 7372800 | bytes 19464192 | tf_op jit(solution)/shard_map/sub | solution.py:132
  215.8 6.7 %all-to-all-start.3 = ((f32[16,2,12,1,128]{4,3,2,1,0:T(1,128)}), f32[16,2,12,1,128]{4,3,2,1,0:T(1,128)}, u32[]{:S(2)}, u32[]{:S(2)}) async-start(f32[16,2,12,1,128]{4,3,2,1,0:T(1,128)} %stack.29), calls=%async_computation.3 | async-start | bytes 393216 | tf_op jit(solution)/shard_map/all_to_all | solution.py:235
  222.4 6.4 %collective-permute-start.14 = (f32[2,12,1,128]{3,2,1,0:T(1,128)}, f32[2,12,1,128]{3,2,1,0:T(1,128)}, u32[]{:S(2)}, u32[]{:S(2)}) collective-permute-start(f32[2,12,1,128]{3,2,1,0:T(1,128)} %get-tuple-element.56), channel_id=1, source_target_pairs={{1,0},{2,1},{3,2},{4,3},{5,4},{6,5},{7,6},{9,8},{10,9},{11,10},{12... | collective-permute-start | bytes 36872 | tf_op jit(solution)/shard_map/ppermute | solution.py:26
  244.4 3.6 %copy.300 = f32[2,12,1,2048]{1,0,3,2:T(2,128)} copy(f32[2,12,1,2048]{3,2,1,0:T(1,128)} %bitcast.164) | data formatting | bytes 393216 | tf_op jit(solution)/shard_map/jit(_take)/Arg_0.21 | solution.py:237
  261.2 3.8 %multiply_add_fusion = f32[2,12,96,128]{3,2,1,0:T(8,128)S(1)} fusion(f32[2,12,96,128]{3,2,1,0:T(8,128)S(1)} %fusion.23, f32[2,11,96,128]{3,2,1,0:T(8,128)S(1)} %copy-done.41, f32[2,11,96,128]{3,2,1,0:T(8,128)S(1)} %fusion.36, f32[2,11,96,128]{3,2,1,0:T(8,128)S(1)} %copy-done.40, f32[2,11,96,128]{3,2,1,0:T(8,128)S(1)} %copy-done.45, ...), kind=kLoop, calls=%fused_computation.81 | loop fusion | flops 9732096 | bytes 17836480 | tf_op jit(solution)/shard_map/add | solution.py:175
  (350 shorter events, 145.3 us)
Async XLA Ops:
  4.6 51.1 %collective-permute-start.3 = (f32[5,12,1,128]{3,2,1,0:T(1,128)}, f32[5,12,1,128]{3,2,1,0:T(1,128)}, u32[]{:S(2)}, u32[]{:S(2)}) collective-permute-start(f32[5,12,1,128]{3,2,1,0:T(1,128)} %get-tuple-element.38), channel_id=1, source_target_pairs={{0,1},{1,2},{2,3},{3,4},{4,5},{5,6},{6,7},{8,9},{9,10},{10,11},{11... | collective-permute-start | bytes 92168 | tf_op jit(solution)/shard_map/ppermute | solution.py:24
  11.3 48.5 %all-to-all-start = ((f32[16,5,12,1,128]{4,3,2,1,0:T(1,128)}), f32[16,5,12,1,128]{4,3,2,1,0:T(1,128)}, u32[]{:S(2)}, u32[]{:S(2)}) async-start(f32[16,5,12,1,128]{4,3,2,1,0:T(1,128)} %stack.26), calls=%async_computation | async-start | bytes 983040 | tf_op jit(solution)/shard_map/all_to_all | solution.py:235
  17.6 52.9 %collective-permute-start.2 = (f32[5,12,1,128]{1,0,3,2:T(8,128)}, f32[5,12,1,128]{1,0,3,2:T(8,128)}, u32[]{:S(2)}, u32[]{:S(2)}) collective-permute-start(f32[5,12,1,128]{1,0,3,2:T(8,128)} %copy.309), channel_id=1, source_target_pairs={{1,0},{2,1},{3,2},{4,3},{5,4},{6,5},{7,6},{9,8},{10,9},{11,10},{12... | collective-permute-start | bytes 92168 | tf_op jit(solution)/shard_map/ppermute | solution.py:26
  29.3 16.2 %collective-permute-start = (f32[5,12,96,1]{2,1,0,3:T(8,128)}, f32[5,12,96,1]{2,1,0,3:T(8,128)}, u32[]{:S(2)}, u32[]{:S(2)}) collective-permute-start(f32[5,12,96,1]{2,1,0,3:T(8,128)} %copy.307), channel_id=1, source_target_pairs={{8,0},{16,8},{24,16},{32,24},{40,32},{48,40},{56,48},{64,56},{72,6... | collective-permute-start | bytes 69128 | tf_op jit(solution)/shard_map/ppermute | solution.py:26
  33.4 17.8 %collective-permute-start.1 = (f32[5,12,96,1]{2,1,0,3:T(8,128)}, f32[5,12,96,1]{2,1,0,3:T(8,128)}, u32[]{:S(2)}, u32[]{:S(2)}) collective-permute-start(f32[5,12,96,1]{2,1,0,3:T(8,128)} %copy.308), channel_id=1, source_target_pairs={{0,8},{8,16},{16,24},{24,32},{32,40},{40,48},{48,56},{56,64},{64,7... | collective-permute-start | bytes 69128 | tf_op jit(solution)/shard_map/ppermute | solution.py:24
  43.4 38.5 %copy-start.12 = (f32[12,96,128]{2,1,0:T(8,128)}, f32[12,96,128]{2,1,0:T(8,128)S(1)}, u32[]{:S(2)}) copy-start(f32[12,96,128]{2,1,0:T(8,128)S(1)} %fusion.83) | copy-start | bytes 1769476
  45.5 184.7 %copy-start.100 = (pred[128]{0:T(512)(128)(4,1)}, pred[128]{0:T(512)(128)(4,1)S(1)}, u32[]{:S(2)}) copy-start(pred[128]{0:T(512)(128)(4,1)S(1)} %get-tuple-element.90) | copy-start | bytes 388
  45.5 186.9 %copy-start.98 = (pred[128]{0:T(512)(128)(4,1)}, pred[128]{0:T(512)(128)(4,1)S(1)}, u32[]{:S(2)}) copy-start(pred[128]{0:T(512)(128)(4,1)S(1)} %get-tuple-element.89) | copy-start | bytes 388
  91.4 24.0 %collective-permute-start.7 = (f32[2,12,1,128]{3,2,1,0:T(1,128)}, f32[2,12,1,128]{3,2,1,0:T(1,128)}, u32[]{:S(2)}, u32[]{:S(2)}) collective-permute-start(f32[2,12,1,128]{3,2,1,0:T(1,128)} %get-tuple-element.64), channel_id=1, source_target_pairs={{0,1},{1,2},{2,3},{3,4},{4,5},{5,6},{6,7},{8,9},{9,10},{10,11},{11... | collective-permute-start | bytes 36872 | tf_op jit(solution)/shard_map/ppermute | solution.py:24
  96.9 19.9 %all-to-all-start.1 = ((f32[16,2,12,1,128]{4,3,2,1,0:T(1,128)}), f32[16,2,12,1,128]{4,3,2,1,0:T(1,128)}, u32[]{:S(2)}, u32[]{:S(2)}) async-start(f32[16,2,12,1,128]{4,3,2,1,0:T(1,128)} %stack.27), calls=%async_computation.1 | async-start | bytes 393216 | tf_op jit(solution)/shard_map/all_to_all | solution.py:235
  103.4 19.3 %collective-permute-start.6 = (f32[2,12,1,128]{3,2,1,0:T(1,128)}, f32[2,12,1,128]{3,2,1,0:T(1,128)}, u32[]{:S(2)}, u32[]{:S(2)}) collective-permute-start(f32[2,12,1,128]{3,2,1,0:T(1,128)} %get-tuple-element.65), channel_id=1, source_target_pairs={{1,0},{2,1},{3,2},{4,3},{5,4},{6,5},{7,6},{9,8},{10,9},{11,10},{12... | collective-permute-start | bytes 36872 | tf_op jit(solution)/shard_map/ppermute | solution.py:26
  109.0 4.5 %collective-permute-start.4 = (f32[2,12,96,1]{2,0,3,1:T(2,128)}, f32[2,12,96,1]{2,0,3,1:T(2,128)}, u32[]{:S(2)}, u32[]{:S(2)}) collective-permute-start(f32[2,12,96,1]{2,0,3,1:T(2,128)} %copy.250), channel_id=1, source_target_pairs={{8,0},{16,8},{24,16},{32,24},{40,32},{48,40},{56,48},{64,56},{72,6... | collective-permute-start | bytes 27656 | tf_op jit(solution)/shard_map/ppermute | solution.py:26
  110.5 4.4 %collective-permute-start.5 = (f32[2,12,96,1]{2,0,3,1:T(2,128)}, f32[2,12,96,1]{2,0,3,1:T(2,128)S(1)}, u32[]{:S(2)}, u32[]{:S(2)}) collective-permute-start(f32[2,12,96,1]{2,0,3,1:T(2,128)} %copy.252), channel_id=1, source_target_pairs={{0,8},{8,16},{16,24},{24,32},{32,40},{40,48},{48,56},{56,64},{64,7... | collective-permute-start | bytes 27656 | tf_op jit(solution)/shard_map/ppermute | solution.py:24
  138.2 45.2 %copy-start.2 = (f32[2,12,96,128]{3,2,1,0:T(8,128)}, f32[2,12,96,128]{3,2,1,0:T(8,128)S(1)}, u32[]{:S(2)}) copy-start(f32[2,12,96,128]{3,2,1,0:T(8,128)S(1)} %fusion.18) | copy-start | bytes 3538948
  149.0 25.4 %collective-permute-start.8 = (f32[4,12,96,1]{2,0,3,1:T(4,128)}, f32[4,12,96,1]{2,0,3,1:T(4,128)}, u32[]{:S(2)}, u32[]{:S(2)}) collective-permute-start(f32[4,12,96,1]{2,0,3,1:T(4,128)} %copy.310), channel_id=1, source_target_pairs={{8,0},{16,8},{24,16},{32,24},{40,32},{48,40},{56,48},{64,56},{72,6... | collective-permute-start | bytes 55304 | tf_op jit(solution)/shard_map/ppermute | solution.py:26
  155.8 19.3 %collective-permute-start.9 = (f32[4,12,96,1]{2,0,3,1:T(4,128)}, f32[4,12,96,1]{2,0,3,1:T(4,128)}, u32[]{:S(2)}, u32[]{:S(2)}) collective-permute-start(f32[4,12,96,1]{2,0,3,1:T(4,128)} %copy.311), channel_id=1, source_target_pairs={{0,8},{8,16},{16,24},{24,32},{32,40},{40,48},{48,56},{56,64},{64,7... | collective-permute-start | bytes 55304 | tf_op jit(solution)/shard_map/ppermute | solution.py:24
  157.3 25.4 %collective-permute-start.11 = (f32[4,12,1,128]{3,2,1,0:T(1,128)}, f32[4,12,1,128]{3,2,1,0:T(1,128)}, u32[]{:S(2)}, u32[]{:S(2)}) collective-permute-start(f32[4,12,1,128]{3,2,1,0:T(1,128)} %get-tuple-element.44), channel_id=1, source_target_pairs={{0,1},{1,2},{2,3},{3,4},{4,5},{5,6},{6,7},{8,9},{9,10},{10,11},{11... | collective-permute-start | bytes 73736 | tf_op jit(solution)/shard_map/ppermute | solution.py:24
  161.3 24.9 %all-to-all-start.2 = ((f32[16,4,12,1,128]{4,1,2,3,0:T(4,128)}), f32[16,4,12,1,128]{4,1,2,3,0:T(4,128)}, u32[]{:S(2)}, u32[]{:S(2)}) async-start(f32[16,4,12,1,128]{4,1,2,3,0:T(4,128)} %stack.28), calls=%async_computation.2 | async-start | bytes 786432 | tf_op jit(solution)/shard_map/all_to_all | solution.py:235
  168.7 25.1 %collective-permute-start.10 = (f32[4,12,1,128]{3,0,1,2:T(4,128)}, f32[4,12,1,128]{3,0,1,2:T(4,128)}, u32[]{:S(2)}, u32[]{:S(2)}) collective-permute-start(f32[4,12,1,128]{3,0,1,2:T(4,128)} %copy.312), channel_id=1, source_target_pairs={{1,0},{2,1},{3,2},{4,3},{5,4},{6,5},{7,6},{9,8},{10,9},{11,10},{12... | collective-permute-start | bytes 73736 | tf_op jit(solution)/shard_map/ppermute | solution.py:26
  206.8 22.1 %collective-permute-start.12 = (f32[2,12,96,1]{2,0,3,1:T(2,128)}, f32[2,12,96,1]{2,0,3,1:T(2,128)}, u32[]{:S(2)}, u32[]{:S(2)}) collective-permute-start(f32[2,12,96,1]{2,0,3,1:T(2,128)} %copy.280), channel_id=1, source_target_pairs={{8,0},{16,8},{24,16},{32,24},{40,32},{48,40},{56,48},{64,56},{72,6... | collective-permute-start | bytes 27656 | tf_op jit(solution)/shard_map/ppermute | solution.py:26
  210.4 19.1 %collective-permute-start.13 = (f32[2,12,96,1]{2,0,3,1:T(2,128)}, f32[2,12,96,1]{2,0,3,1:T(2,128)}, u32[]{:S(2)}, u32[]{:S(2)}) collective-permute-start(f32[2,12,96,1]{2,0,3,1:T(2,128)} %copy.282), channel_id=1, source_target_pairs={{0,8},{8,16},{16,24},{24,32},{32,40},{40,48},{48,56},{56,64},{64,7... | collective-permute-start | bytes 27656 | tf_op jit(solution)/shard_map/ppermute | solution.py:24
  212.3 26.5 %collective-permute-start.15 = (f32[2,12,1,128]{3,2,1,0:T(1,128)}, f32[2,12,1,128]{3,2,1,0:T(1,128)}, u32[]{:S(2)}, u32[]{:S(2)}) collective-permute-start(f32[2,12,1,128]{3,2,1,0:T(1,128)} %get-tuple-element.57), channel_id=1, source_target_pairs={{0,1},{1,2},{2,3},{3,4},{4,5},{5,6},{6,7},{8,9},{9,10},{10,11},{11... | collective-permute-start | bytes 36872 | tf_op jit(solution)/shard_map/ppermute | solution.py:24
  215.8 27.0 %all-to-all-start.3 = ((f32[16,2,12,1,128]{4,3,2,1,0:T(1,128)}), f32[16,2,12,1,128]{4,3,2,1,0:T(1,128)}, u32[]{:S(2)}, u32[]{:S(2)}) async-start(f32[16,2,12,1,128]{4,3,2,1,0:T(1,128)} %stack.29), calls=%async_computation.3 | async-start | bytes 393216 | tf_op jit(solution)/shard_map/all_to_all | solution.py:235
  222.4 30.3 %collective-permute-start.14 = (f32[2,12,1,128]{3,2,1,0:T(1,128)}, f32[2,12,1,128]{3,2,1,0:T(1,128)}, u32[]{:S(2)}, u32[]{:S(2)}) collective-permute-start(f32[2,12,1,128]{3,2,1,0:T(1,128)} %get-tuple-element.56), channel_id=1, source_target_pairs={{1,0},{2,1},{3,2},{4,3},{5,4},{6,5},{7,6},{9,8},{10,9},{11,10},{12... | collective-permute-start | bytes 36872 | tf_op jit(solution)/shard_map/ppermute | solution.py:26
  (101 other events, 547.8 us)
